TPU v7x, 256 devices: a whole 4x4x8 slice. The times are simulated.
256 devices in a mesh: rows: 32 (over y_lo, z, core), protos: 8 (over y_hi, x).
Axes of the slice: x: 4, y: 4 (y_hi: 2, y_lo: 2; y = y_hi * 2 + y_lo), z: 8, core: 2. Of those that a mesh axis runs over, the one named last changes fastest.
Arguments:
- teacher: bfloat16 [2048, 256], P('rows')
- students: bfloat16 [8192, 256], P('rows')
- prototypes: bfloat16 [256, 65536], P(None, 'protos')
- pairing: int32 [8192], P('rows'), may hold values from 0 to 63
- layout: int32 [8192], P('rows'), may hold values from 0 to 31, as said below
Outputs:
- grad_students: float32 [8192, 256], P('rows')
- grad_protos: float32 [256, 65536], P('rows', 'protos')
Inputs may be any that keep to these rules, and one draw needn't show every extreme that they name: `layout`: in each aligned block of 256 rows, every value appears exactly 8 times.
All inputs are finite; a program needn't handle non-finite values.
Results may differ from a plain program's by a relative error of at most 0.0003.
The roundings to bfloat16 on the way count: a program that leaves them out, or rounds other values in their place, can miss the bound.
Values may be sent and summed in bfloat16 or wider, within the bound.
A program may use at most 64 MiB of HBM per device.

v0:
```python
import jax
import jax.numpy as jnp
from jax import lax
from jax.sharding import PartitionSpec as P

PROTOS = 65536
ITERS = 2
epsilon = 1e-06
teacher_temp = 0.07
student_temp = 0.1
loss_scale = 16.0


def body(teacher, students, prototypes, pairing, layout):
    row_devices = lax.axis_size("rows")
    tea_count = teacher.shape[0]
    total_teachers = tea_count * row_devices
    local_protos = prototypes.shape[1]
    weights = prototypes.astype(jnp.float32)
    w_norm = jnp.sqrt(jnp.sum(weights * weights, 0) + epsilon)
    w_unit = weights / w_norm
    w_unit_b = w_unit.astype(jnp.bfloat16)
    tea_full = teacher.astype(jnp.float32)
    tea_unit_b = (
        tea_full / jnp.sqrt(jnp.sum(tea_full * tea_full, 1, keepdims=True) + epsilon)
    ).astype(jnp.bfloat16)
    exp_scores = jnp.exp(
        jnp.dot(tea_unit_b, w_unit_b, preferred_element_type=jnp.float32) / teacher_temp
    )
    row_factor = jnp.ones((tea_count,), jnp.float32)
    col_factor = jnp.ones((local_protos,), jnp.float32)
    for sweep in range(ITERS):
        colsum = lax.psum(jnp.sum(exp_scores * row_factor[:, None], 0), "rows")
        col_factor = 1.0 / (PROTOS * colsum)
        rowsum = lax.psum(jnp.sum(exp_scores * col_factor[None, :], 1), "protos")
        row_factor = 1.0 / (total_teachers * rowsum)
    send_order = jnp.argsort(layout, stable=True)
    moved_rows, moved_pairs = (
        lax.all_to_all(students[send_order], "rows", split_axis=0, concat_axis=0, tiled=True),
        lax.all_to_all(pairing[send_order], "rows", split_axis=0, concat_axis=0, tiled=True),
    )
    balanced = total_teachers * exp_scores * row_factor[:, None] * col_factor[None, :]
    target_rows = balanced[moved_pairs]
    stu_full = moved_rows.astype(jnp.float32)
    u_norm = jnp.sqrt(jnp.sum(stu_full * stu_full, 1, keepdims=True) + epsilon)
    stu_unit = stu_full / u_norm
    stu_unit_b = stu_unit.astype(jnp.bfloat16)
    logits = jnp.dot(stu_unit_b, w_unit_b, preferred_element_type=jnp.float32) / student_temp
    exp_logits = jnp.exp(logits)
    denominator = lax.psum(jnp.sum(exp_logits, 1), "protos")
    grad_logits = (
        loss_scale / student_temp * (exp_logits / denominator[:, None] - target_rows)
    ).astype(jnp.bfloat16)
    partial_unit = jnp.einsum(
        "sk,dk->sd", grad_logits, w_unit_b, preferred_element_type=jnp.float32
    )
    grad_unit = lax.psum(partial_unit, "protos")
    grad_rows = (grad_unit - stu_unit * jnp.sum(stu_unit * grad_unit, 1, keepdims=True)) / u_norm
    returned = lax.all_to_all(grad_rows, "rows", split_axis=0, concat_axis=0, tiled=True)
    grad_students = returned[jnp.argsort(send_order)]
    feature_share = prototypes.shape[0] // row_devices
    first_feature = lax.axis_index("rows") * feature_share
    grad_share = lax.psum_scatter(
        jnp.einsum("sd,sk->dk", stu_unit_b, grad_logits, preferred_element_type=jnp.float32),
        "rows",
        scatter_dimension=0,
        tiled=True,
    )
    unit_share = lax.dynamic_slice_in_dim(w_unit, first_feature, feature_share, 0)
    inner = lax.psum(jnp.sum(unit_share * grad_share, 0), "rows")
    grad_protos = (grad_share - unit_share * inner[None, :]) / w_norm
    return (grad_students, grad_protos)


def solution(mesh):
    in_specs = (P("rows", None), P("rows", None), P(None, "protos"), P("rows"), P("rows"))
    out_specs = (P("rows", None), P("rows", "protos"))
    return jax.shard_map(body, mesh=mesh, in_specs=in_specs, out_specs=out_specs, check_vma=False)
```

profile of v0, /device:TPU:16, one launch (start us, length us, event | category | flops | bytes accessed | tf_op | source)
XLA Modules:
  0.0 580.0 jit_solution(10090649880890800840)
XLA Ops:
  8.0 0.0 copy-start
  8.0 0.0 copy-start.5
  8.0 3.9 sort.34
  11.9 2.0 gather_fusion.1
  13.9 0.7 all_to_all.24
  14.6 9.6 %all-to-all-start.1 = ((s32[32,8,1]{1,2,0:T(1,128)}), s32[32,8,1]{1,2,0:T(1,128)S(1)}, u32[]{:S(2)}, u32[]{:S(2)}) async-start(s32[32,8,1]{1,2,0:T(1,128)} %bitcast.2), calls=%async_computation.1 | async-start | bytes 32768 | tf_op jit(solution)/shard_map/all_to_all | solution.py:40
  24.2 0.0 copy-start.2
  24.2 3.2 fusion.2
  27.4 0.0 copy-done.5
  27.4 0.1 fusion.5
  27.6 0.1 copy-done.2
  27.6 1.3 fusion.18
  29.0 0.0 copy-start.1
  29.0 108.1 %psum.50 = f32[8192]{0:T(1024)S(1)} all-reduce(f32[8192]{0:T(1024)S(1)} %get-tuple-element.8), channel_id=1, replica_groups=mesh['rows'=32,'protos'=8] {'rows'}, use_global_device_ids=true, to_apply=%region_7.0 | all-reduce | flops 8192 | bytes 65536 | tf_op jit(solution)/shard_map/psum | solution.py:33
  137.1 0.2 multiply_reduce_fusion.2
  137.3 21.8 %psum.51 = f32[64]{0:T(128)S(1)} all-reduce(f32[64]{0:T(128)S(1)} %multiply_reduce_fusion.2), channel_id=1, replica_groups=mesh['rows'=32,'protos'=8] {'protos'}, use_global_device_ids=true, to_apply=%region_9.0 | all-reduce | flops 64 | bytes 512 | tf_op jit(solution)/shard_map/psum | solution.py:35
  159.1 0.3 multiply_reduce_fusion.1
  159.4 104.4 %psum.52 = f32[8192]{0:T(1024)S(1)} all-reduce(f32[8192]{0:T(1024)S(1)} %multiply_reduce_fusion.1), channel_id=1, replica_groups=mesh['rows'=32,'protos'=8] {'rows'}, use_global_device_ids=true, to_apply=%region_11.12 | all-reduce | flops 8192 | bytes 65536 | tf_op jit(solution)/shard_map/psum | solution.py:33
  263.8 0.2 multiply_reduce_fusion
  264.0 0.0 copy-done
  264.0 1.8 gather_fusion
  265.8 0.0 all-to-all-done.1
  265.8 3.9 all-to-all-start
  269.7 0.0 all-reduce.3.cloned.1.call-start
  269.8 0.5 broadcast.97
  270.3 0.7 reduce.4
  271.0 0.1 all_to_all.26
  271.1 9.0 %all-to-all-done = bf16[32,8,256]{2,1,0:T(8,128)(2,1)S(1)} async-done(((bf16[32,8,256]{2,1,0:T(8,128)(2,1)}), bf16[32,8,256]{2,1,0:T(8,128)(2,1)S(1)}, u32[]{:S(2)}, u32[]{:S(2)}) %all-to-all-start) | async-done | bytes 131104 | tf_op jit(solution)/shard_map/all_to_all | solution.py:39
  280.1 0.1 fusion.4
  280.3 0.1 sqrt.27
  280.3 7.6 %fusion.19 = (f32[256]{0:T(256)S(1)}, f32[256,8192]{1,0:T(8,128)}) fusion(f32[8192]{0:T(1024)S(1)} %add_sqrt_fusion, bf16[256,8192]{1,0:T(8,128)(2,1)} %param.7, f32[256]{0:T(256)S(1)} %sqrt.27, bf16[32,8,256]{2,1,0:T(8,128)(2,1)S(1)} %all-to-all-done), kind=kOutput, calls=%fused_computation.50 | convolution fusion | flops 1084423936 | bytes 12748800 | tf_op jit(solution)/shard_map/dot_general | solution.py:48
  288.0 0.0 copy-done.1
  288.0 19.1 %all-reduce = (f32[64]{0:T(128)S(1)}, f32[256]{0:T(256)S(1)}) all-reduce(f32[64]{0:T(128)S(1)} %multiply_reduce_fusion, f32[256]{0:T(256)S(1)} %get-tuple-element.10), channel_id=1, replica_groups=mesh['rows'=32,'protos'=8] {'protos'}, use_global_device_ids=true, to_apply=%region_13.14 | all-reduce | flops 320 | bytes 2560 | tf_op jit(solution)/shard_map/psum | solution.py:35
  307.1 1.9 multiply_multiply_fusion
  309.0 6.2 %gather_fusion.2 = f32[256,8192]{1,0:T(8,128)} fusion(f32[64,8192]{1,0:T(8,128)S(1)} %multiply_multiply_fusion, s32[1024]{0:T(1024)S(1)} %pad_clamp_fusion.1), kind=kCustom, calls=%fused_computation.2 | custom fusion | bytes 16778240 | tf_op jit(solution)/shard_map/gather | solution.py:43
  315.2 0.0 copy-start.3
  315.2 6.7 %multiply_convert_fusion = bf16[256,8192]{1,0:T(8,128)(2,1)S(1)} fusion(f32[256,8192]{1,0:T(8,128)} %gather_fusion.2, f32[256,8192]{1,0:T(8,128)} %get-tuple-element.11, f32[256]{0:T(256)S(1)} %get-tuple-element.7), kind=kLoop, calls=%fused_computation.11 | loop fusion | flops 8388608 | bytes 20972544 | tf_op jit(solution)/shard_map/convert_element_type | solution.py:53
  321.9 0.0 copy-start.4
  321.9 2.0 copy-done.4
  323.8 0.0 copy-done.3
  323.8 2.0 fusion.12
  325.8 0.0 all-reduce.3.cloned.1.call-update
  325.9 0.0 reduce-scatter.2.cloned.1.call-start
  325.9 6.8 %fusion.7 = f32[256,8192]{1,0:T(8,128)} fusion(bf16[256,8192]{1,0:T(8,128)(2,1)} %copy-done.4, bf16[32,8,256]{2,1,0:T(8,128)(2,1)S(1)} %all-to-all-done, f32[256]{0:T(256)S(1)} %sqrt.27), kind=kOutput, calls=%fused_computation.28 | convolution fusion | flops 1073938432 | bytes 12715008 | tf_op jit(solution)/shard_map/sd,sk->dk/dot_general | solution.py:64
  332.7 0.0 reduce-scatter.2.cloned.1.call-update
  332.7 76.2 %all-reduce.3.cloned.1.call-done = f32[256,256]{1,0:T(8,128)} async-done(((f32[256,256]{1,0:T(8,128)}), f32[256,256]{1,0:T(8,128)}) %all-reduce.3.cloned.1.call-update) | async-done | bytes 262160 | tf_op jit(solution)/shard_map/psum | solution.py:57
  409.0 1.1 multiply_reduce_fusion.4
  410.1 1.8 divide_bitcast_fusion
  411.9 8.8 %all-to-all-start.2 = ((f32[32,8,256]{2,1,0:T(8,128)}), f32[32,8,256]{2,1,0:T(8,128)S(1)}, u32[]{:S(2)}, u32[]{:S(2)}) async-start(f32[32,8,256]{2,1,0:T(8,128)} %divide_bitcast_fusion), calls=%async_computation.2 | async-start | bytes 524288 | tf_op jit(solution)/shard_map/all_to_all | solution.py:59
  420.7 6.5 %convert_divide_fusion = f32[256,8192]{1,0:T(8,128)} fusion(bf16[256,8192]{1,0:T(8,128)(2,1)} %param.7, f32[8192]{0:T(1024)S(1)} %add_sqrt_fusion), kind=kLoop, calls=%fused_computation.6 | loop fusion | flops 4194304 | bytes 12615680 | tf_op jit(solution)/shard_map/div | solution.py:21
  427.2 3.2 sort.35
  430.4 4.6 all-to-all-done.2
  435.0 1.7 gather_fusion.3
  436.7 28.6 %reduce-scatter.2.cloned.1.call-done = f32[8,8192]{1,0:T(8,128)} async-done(((f32[256,8192]{1,0:T(8,128)}), f32[8,8192]{1,0:T(8,128)}) %reduce-scatter.2.cloned.1.call-update) | async-done | bytes 262160 | tf_op jit(solution)/shard_map/reduce_scatter | solution.py:63
  465.2 1.1 multiply_reduce_fusion.3
  466.4 104.4 %psum.55 = f32[8192]{0:T(1024)S(1)} all-reduce(f32[8192]{0:T(1024)S(1)} %multiply_reduce_fusion.3), channel_id=1, replica_groups=mesh['rows'=32,'protos'=8] {'rows'}, use_global_device_ids=true, to_apply=%region_19.20 | all-reduce | flops 8192 | bytes 65536 | tf_op jit(solution)/shard_map/psum | solution.py:70
  570.8 1.8 subtract_divide_fusion
  (15 shorter events, 0.1 us)
Async XLA Ops:
  8.0 256.0 %copy-start = (bf16[256,256]{1,0:T(8,128)(2,1)S(1)}, bf16[256,256]{1,0:T(8,128)(2,1)}, u32[]{:S(2)}) copy-start(bf16[256,256]{1,0:T(8,128)(2,1)} %param.6) | copy-start | bytes 393220
  8.0 19.4 %copy-start.5 = (bf16[64,256]{1,0:T(8,128)(2,1)S(1)}, bf16[64,256]{1,0:T(8,128)(2,1)}, u32[]{:S(2)}) copy-start(bf16[64,256]{1,0:T(8,128)(2,1)} %param.5) | copy-start | bytes 98308
  14.6 251.2 %all-to-all-start.1 = ((s32[32,8,1]{1,2,0:T(1,128)}), s32[32,8,1]{1,2,0:T(1,128)S(1)}, u32[]{:S(2)}, u32[]{:S(2)}) async-start(s32[32,8,1]{1,2,0:T(1,128)} %bitcast.2), calls=%async_computation.1 | async-start | bytes 32768 | tf_op jit(solution)/shard_map/all_to_all | solution.py:40
  24.2 3.5 copy-start.2
  29.0 259.0 %copy-start.1 = (f32[64,8192]{1,0:T(8,128)}, f32[64,8192]{1,0:T(8,128)S(1)}, u32[]{:S(2)}) copy-start(f32[64,8192]{1,0:T(8,128)S(1)} %get-tuple-element.9) | copy-start | bytes 6291460
  265.8 14.3 %all-to-all-start = ((bf16[32,8,256]{2,1,0:T(8,128)(2,1)}), bf16[32,8,256]{2,1,0:T(8,128)(2,1)S(1)}, u32[]{:S(2)}, u32[]{:S(2)}) async-start(bf16[32,8,256]{2,1,0:T(8,128)(2,1)} %bitcast), calls=%async_computation | async-start | bytes 262144 | tf_op jit(solution)/shard_map/all_to_all | solution.py:39
  269.7 139.2 %all-reduce.3.cloned.1.call-start = ((), (), s32[]{:S(2)}) async-start(), calls=%async_computation.4 | async-start | bytes 524288 | tf_op jit(solution)/shard_map/psum | solution.py:57
  315.2 8.7 %copy-start.3 = (bf16[256,8192]{1,0:T(8,128)(2,1)S(1)}, bf16[256,8192]{1,0:T(8,128)(2,1)}, u32[]{:S(2)}) copy-start(bf16[256,8192]{1,0:T(8,128)(2,1)} %param.7) | copy-start | bytes 12582916
  321.9 2.0 copy-start.4
  325.9 139.4 %reduce-scatter.2.cloned.1.call-start = ((), (), s32[]{:S(2)}) async-start(), calls=%async_computation.5 | async-start | bytes 8650752 | tf_op jit(solution)/shard_map/reduce_scatter | solution.py:63
  411.9 23.1 %all-to-all-start.2 = ((f32[32,8,256]{2,1,0:T(8,128)}), f32[32,8,256]{2,1,0:T(8,128)S(1)}, u32[]{:S(2)}, u32[]{:S(2)}) async-start(f32[32,8,256]{2,1,0:T(8,128)} %divide_bitcast_fusion), calls=%async_computation.2 | async-start | bytes 524288 | tf_op jit(solution)/shard_map/all_to_all | solution.py:59
Sparse Core Ops, SparseCore 0:
  326.0 82.9 all-reduce.2
Sparse Core Ops, SparseCore 1:
  332.8 132.4 reduce-scatter.1
where the time goes:
time: 581 us; the launch traced here: 580 us
  blocking collectives  358 us (62%)
  waiting for transfers between devices  118 us (20%)
  other arithmetic  32.9 us (6%)
  starting transfers between devices  22.3 us (4%)
  matrix products  17.7 us (3%)
  between operations  15.7 us (3%)
  local copies, waits for them, and re-layouts  15.1 us (3%)
    psum x2, blocking collectives, body(): colsum = lax.psum(jnp.sum(exp_scores * row_factor[:, None], 0), 'rows')  212 us
    psum x1, blocking collectives, body(): inner = lax.psum(jnp.sum(unit_share * grad_share, 0), 'rows')  104 us
    psum x1, waiting for transfers between devices, body(): grad_unit = lax.psum(partial_unit, 'protos')  76.2 us
    psum x2, blocking collectives, body(): rowsum = lax.psum(jnp.sum(exp_scores * col_factor[None, :], 1), 'protos')  40.9 us
    reduce_scatter x1, waiting for transfers between devices, body(): lax.psum_scatter(jnp.einsum('sd,sk->dk', stu_unit_b, grad_logits, preferr...  28.6 us
  transfers between devices with their start and end apart: 5, of which 4 were waited for; matrix products, arithmetic and copies ran while one was open for 5% of the time, Pallas kernels for 0%

commit v1 on v0

--- a/solution.py
+++ b/solution.py
@@ -54,7 +54,7 @@
     partial_unit = jnp.einsum(
         "sk,dk->sd", grad_logits, w_unit_b, preferred_element_type=jnp.float32
     )
-    grad_unit = lax.psum(partial_unit, "protos")
+    grad_unit = jnp.sum(lax.all_gather(partial_unit, "protos"), axis=0)
     grad_rows = (grad_unit - stu_unit * jnp.sum(stu_unit * grad_unit, 1, keepdims=True)) / u_norm
     returned = lax.all_to_all(grad_rows, "rows", split_axis=0, concat_axis=0, tiled=True)
     grad_students = returned[jnp.argsort(send_order)]

time: 581 us -> 580 us (level)
    psum x1 -> x0, waiting for transfers between devices: 76.2 us -> none  [body(): grad_unit = lax.psum(partial_unit, 'protos')]
    all_gather x0 -> x1, waiting for transfers between devices: none -> 52.1 us  [body(): grad_unit = jnp.sum(lax.all_gather(partial_unit, 'protos'), axis=0)]
    reduce_scatter x1, waiting for transfers between devices: 28.6 us -> 50.4 us  [body(): lax.psum_scatter(jnp.einsum('sd,sk->dk', stu_unit_b, grad_logits, preferr...]
where the time goes in v1:
time: 580 us; the launch traced here: 577 us
  blocking collectives  358 us (62%)
  waiting for transfers between devices  116 us (20%)
  other arithmetic  33.7 us (6%)
  starting transfers between devices  20.8 us (4%)
  matrix products  17.7 us (3%)
  between operations  15.7 us (3%)
  local copies, waits for them, and re-layouts  15.1 us (3%)
    psum x2, blocking collectives, body(): colsum = lax.psum(jnp.sum(exp_scores * row_factor[:, None], 0), 'rows')  212 us
    psum x1, blocking collectives, body(): inner = lax.psum(jnp.sum(unit_share * grad_share, 0), 'rows')  105 us
    all_gather x1, waiting for transfers between devices, body(): grad_unit = jnp.sum(lax.all_gather(partial_unit, 'protos'), axis=0)  52.1 us
    reduce_scatter x1, waiting for transfers between devices, body(): lax.psum_scatter(jnp.einsum('sd,sk->dk', stu_unit_b, grad_logits, preferr...  50.4 us
    psum x2, blocking collectives, body(): rowsum = lax.psum(jnp.sum(exp_scores * col_factor[None, :], 1), 'protos')  40.9 us
  transfers between devices with their start and end apart: 5, of which 4 were waited for; matrix products, arithmetic and copies ran while one was open for 5% of the time, Pallas kernels for 0%

profile of v1, /device:TPU:16, one launch (start us, length us, event | category | flops | bytes accessed | tf_op | source)
XLA Modules:
  0.0 577.2 jit_solution(10180483415915705588)
XLA Ops:
  8.0 0.0 copy-start
  8.0 0.0 copy-start.5
  8.0 3.9 sort.34
  11.9 2.0 gather_fusion.1
  13.9 0.7 all_to_all.22
  14.6 9.6 %all-to-all-start.1 = ((s32[32,8,1]{1,2,0:T(1,128)}), s32[32,8,1]{1,2,0:T(1,128)S(1)}, u32[]{:S(2)}, u32[]{:S(2)}) async-start(s32[32,8,1]{1,2,0:T(1,128)} %bitcast.2), calls=%async_computation.1 | async-start | bytes 32768 | tf_op jit(solution)/shard_map/all_to_all | solution.py:40
  24.2 0.0 copy-start.2
  24.2 3.2 fusion.3
  27.4 0.0 copy-done.5
  27.4 0.1 fusion.12
  27.6 0.1 copy-done.2
  27.6 1.3 fusion.23
  29.0 0.0 copy-start.1
  29.0 108.1 %psum.43 = f32[8192]{0:T(1024)S(1)} all-reduce(f32[8192]{0:T(1024)S(1)} %get-tuple-element.8), channel_id=1, replica_groups=mesh['rows'=32,'protos'=8] {'rows'}, use_global_device_ids=true, to_apply=%region_7.0 | all-reduce | flops 8192 | bytes 65536 | tf_op jit(solution)/shard_map/psum | solution.py:33
  137.1 0.2 multiply_reduce_fusion.2
  137.3 21.8 %psum.44 = f32[64]{0:T(128)S(1)} all-reduce(f32[64]{0:T(128)S(1)} %multiply_reduce_fusion.2), channel_id=1, replica_groups=mesh['rows'=32,'protos'=8] {'protos'}, use_global_device_ids=true, to_apply=%region_9.0 | all-reduce | flops 64 | bytes 512 | tf_op jit(solution)/shard_map/psum | solution.py:35
  159.1 0.3 multiply_reduce_fusion.1
  159.4 104.4 %psum.45 = f32[8192]{0:T(1024)S(1)} all-reduce(f32[8192]{0:T(1024)S(1)} %multiply_reduce_fusion.1), channel_id=1, replica_groups=mesh['rows'=32,'protos'=8] {'rows'}, use_global_device_ids=true, to_apply=%region_11.12 | all-reduce | flops 8192 | bytes 65536 | tf_op jit(solution)/shard_map/psum | solution.py:33
  263.8 0.2 multiply_reduce_fusion
  264.0 0.0 copy-done
  264.0 1.8 gather_fusion
  265.8 0.0 all-to-all-done.1
  265.8 3.9 all-to-all-start
  269.7 0.0 all-gather.3.cloned.1.call-start
  269.8 0.5 broadcast.106
  270.3 0.7 reduce.5
  271.0 0.1 all_to_all.24
  271.1 9.0 %all-to-all-done = bf16[32,8,256]{2,1,0:T(8,128)(2,1)S(1)} async-done(((bf16[32,8,256]{2,1,0:T(8,128)(2,1)}), bf16[32,8,256]{2,1,0:T(8,128)(2,1)S(1)}, u32[]{:S(2)}, u32[]{:S(2)}) %all-to-all-start) | async-done | bytes 131104 | tf_op jit(solution)/shard_map/all_to_all | solution.py:39
  280.1 0.1 fusion.9
  280.3 0.1 sqrt.28
  280.3 7.6 %fusion.24 = (f32[256]{0:T(256)S(1)}, f32[256,8192]{1,0:T(8,128)}) fusion(f32[8192]{0:T(1024)S(1)} %add_sqrt_fusion, bf16[256,8192]{1,0:T(8,128)(2,1)} %param.7, bf16[32,8,256]{2,1,0:T(8,128)(2,1)S(1)} %all-to-all-done, f32[256]{0:T(256)S(1)} %sqrt.28), kind=kOutput, calls=%fused_computation.55 | convolution fusion | flops 1084423936 | bytes 12748800 | tf_op jit(solution)/shard_map/dot_general | solution.py:48
  288.0 0.0 copy-done.1
  288.0 19.1 %all-reduce = (f32[64]{0:T(128)S(1)}, f32[256]{0:T(256)S(1)}) all-reduce(f32[64]{0:T(128)S(1)} %multiply_reduce_fusion, f32[256]{0:T(256)S(1)} %get-tuple-element.10), channel_id=1, replica_groups=mesh['rows'=32,'protos'=8] {'protos'}, use_global_device_ids=true, to_apply=%region_13.14 | all-reduce | flops 320 | bytes 2560 | tf_op jit(solution)/shard_map/psum | solution.py:35
  307.1 1.9 multiply_multiply_fusion
  309.0 6.2 %gather_fusion.2 = f32[256,8192]{1,0:T(8,128)} fusion(f32[64,8192]{1,0:T(8,128)S(1)} %multiply_multiply_fusion, s32[1024]{0:T(1024)S(1)} %pad_clamp_fusion.1), kind=kCustom, calls=%fused_computation.2 | custom fusion | bytes 16778240 | tf_op jit(solution)/shard_map/gather | solution.py:43
  315.2 0.0 copy-start.3
  315.2 6.7 %multiply_convert_fusion = bf16[256,8192]{1,0:T(8,128)(2,1)S(1)} fusion(f32[256,8192]{1,0:T(8,128)} %gather_fusion.2, f32[256,8192]{1,0:T(8,128)} %get-tuple-element.11, f32[256]{0:T(256)S(1)} %get-tuple-element.7), kind=kLoop, calls=%fused_computation.12 | loop fusion | flops 8388608 | bytes 20972544 | tf_op jit(solution)/shard_map/convert_element_type | solution.py:53
  321.9 0.0 copy-start.4
  321.9 2.0 copy-done.4
  323.8 0.0 copy-done.3
  323.8 2.0 fusion.16
  325.8 0.0 all-gather.3.cloned.1.call-update
  325.9 0.0 reduce-scatter.2.cloned.1.call-start
  325.9 6.8 %fusion.20 = f32[256,8192]{1,0:T(8,128)} fusion(bf16[256,8192]{1,0:T(8,128)(2,1)} %copy-done.4, bf16[32,8,256]{2,1,0:T(8,128)(2,1)S(1)} %all-to-all-done, f32[256]{0:T(256)S(1)} %sqrt.28), kind=kOutput, calls=%fused_computation.53 | convolution fusion | flops 1073938432 | bytes 12715008 | tf_op jit(solution)/shard_map/sd,sk->dk/dot_general | solution.py:64
  332.7 0.0 reduce-scatter.2.cloned.1.call-update
  332.7 52.1 %all-gather.3.cloned.1.call-done = f32[2048,256]{1,0:T(8,128)} async-done(((f32[256,256]{1,0:T(8,128)}), f32[2048,256]{1,0:T(8,128)}) %all-gather.3.cloned.1.call-update) | async-done | bytes 2097168 | tf_op jit(solution)/shard_map/all_gather | solution.py:57
  384.9 1.8 reduce_sum.109
  386.7 2.0 fusion.6
  388.6 7.3 %all-to-all-start.2 = ((f32[32,8,256]{2,1,0:T(8,128)}), f32[32,8,256]{2,1,0:T(8,128)S(1)}, u32[]{:S(2)}, u32[]{:S(2)}) async-start(f32[32,8,256]{2,1,0:T(8,128)} %fusion.6), calls=%async_computation.2 | async-start | bytes 524288 | tf_op jit(solution)/shard_map/all_to_all | solution.py:59
  396.0 6.5 %convert_divide_fusion = f32[256,8192]{1,0:T(8,128)} fusion(bf16[256,8192]{1,0:T(8,128)(2,1)} %param.7, f32[8192]{0:T(1024)S(1)} %add_sqrt_fusion), kind=kLoop, calls=%fused_computation.7 | loop fusion | flops 4194304 | bytes 12615680 | tf_op jit(solution)/shard_map/div | solution.py:21
  402.4 3.2 sort.35
  405.6 4.4 all-to-all-done.2
  410.0 1.7 gather_fusion.3
  411.6 50.4 %reduce-scatter.2.cloned.1.call-done = f32[8,8192]{1,0:T(8,128)} async-done(((f32[256,8192]{1,0:T(8,128)}), f32[8,8192]{1,0:T(8,128)}) %reduce-scatter.2.cloned.1.call-update) | async-done | bytes 262160 | tf_op jit(solution)/shard_map/reduce_scatter | solution.py:63
  462.0 1.1 multiply_reduce_fusion.3
  463.1 104.9 %psum.47 = f32[8192]{0:T(1024)S(1)} all-reduce(f32[8192]{0:T(1024)S(1)} %multiply_reduce_fusion.3), channel_id=1, replica_groups=mesh['rows'=32,'protos'=8] {'rows'}, use_global_device_ids=true, to_apply=%region_19.20 | all-reduce | flops 8192 | bytes 65536 | tf_op jit(solution)/shard_map/psum | solution.py:70
  568.0 1.8 subtract_divide_fusion
  (15 shorter events, 0.1 us)
Async XLA Ops:
  8.0 256.0 %copy-start = (bf16[256,256]{1,0:T(8,128)(2,1)S(1)}, bf16[256,256]{1,0:T(8,128)(2,1)}, u32[]{:S(2)}) copy-start(bf16[256,256]{1,0:T(8,128)(2,1)} %param.6) | copy-start | bytes 393220
  8.0 19.4 %copy-start.5 = (bf16[64,256]{1,0:T(8,128)(2,1)S(1)}, bf16[64,256]{1,0:T(8,128)(2,1)}, u32[]{:S(2)}) copy-start(bf16[64,256]{1,0:T(8,128)(2,1)} %param.5) | copy-start | bytes 98308
  14.6 251.2 %all-to-all-start.1 = ((s32[32,8,1]{1,2,0:T(1,128)}), s32[32,8,1]{1,2,0:T(1,128)S(1)}, u32[]{:S(2)}, u32[]{:S(2)}) async-start(s32[32,8,1]{1,2,0:T(1,128)} %bitcast.2), calls=%async_computation.1 | async-start | bytes 32768 | tf_op jit(solution)/shard_map/all_to_all | solution.py:40
  24.2 3.5 copy-start.2
  29.0 259.0 %copy-start.1 = (f32[64,8192]{1,0:T(8,128)}, f32[64,8192]{1,0:T(8,128)S(1)}, u32[]{:S(2)}) copy-start(f32[64,8192]{1,0:T(8,128)S(1)} %get-tuple-element.9) | copy-start | bytes 6291460
  265.8 14.3 %all-to-all-start = ((bf16[32,8,256]{2,1,0:T(8,128)(2,1)}), bf16[32,8,256]{2,1,0:T(8,128)(2,1)S(1)}, u32[]{:S(2)}, u32[]{:S(2)}) async-start(bf16[32,8,256]{2,1,0:T(8,128)(2,1)} %bitcast), calls=%async_computation | async-start | bytes 262144 | tf_op jit(solution)/shard_map/all_to_all | solution.py:39
  269.7 115.1 %all-gather.3.cloned.1.call-start = ((), (), s32[]{:S(2)}) async-start(), calls=%async_computation.5 | async-start | bytes 2359296 | tf_op jit(solution)/shard_map/all_gather | solution.py:57
  315.2 8.7 %copy-start.3 = (bf16[256,8192]{1,0:T(8,128)(2,1)S(1)}, bf16[256,8192]{1,0:T(8,128)(2,1)}, u32[]{:S(2)}) copy-start(bf16[256,8192]{1,0:T(8,128)(2,1)} %param.7) | copy-start | bytes 12582916
  321.9 2.0 copy-start.4
  325.9 136.1 %reduce-scatter.2.cloned.1.call-start = ((), (), s32[]{:S(2)}) async-start(), calls=%async_computation.4 | async-start | bytes 8650752 | tf_op jit(solution)/shard_map/reduce_scatter | solution.py:63
  388.6 21.3 %all-to-all-start.2 = ((f32[32,8,256]{2,1,0:T(8,128)}), f32[32,8,256]{2,1,0:T(8,128)S(1)}, u32[]{:S(2)}, u32[]{:S(2)}) async-start(f32[32,8,256]{2,1,0:T(8,128)} %fusion.6), calls=%async_computation.2 | async-start | bytes 524288 | tf_op jit(solution)/shard_map/all_to_all | solution.py:59
Sparse Core Ops, SparseCore 0:
  326.0 58.8 all-gather.2
Sparse Core Ops, SparseCore 1:
  332.8 129.1 reduce-scatter.1
